TPU v7x, 256 devices: a whole 4x4x8 slice. The times are simulated.
256 devices in a mesh: row: 32 (over z, y_hi, core), col: 8 (over y_lo, x).
Axes of the slice: x: 4, y: 4 (y_hi: 2, y_lo: 2; y = y_hi * 2 + y_lo), z: 8, core: 2. Of those that a mesh axis runs over, the one named last changes fastest.
Arguments:
- obs_summaries: bfloat16 [16384, 256], P(('row', 'col')), may hold values from -6 to 6
- sim_summaries: bfloat16 [8192, 256], P('row'), may hold values from -6 to 6
- neighbours: int32 [16384, 16], P(('row', 'col')), may hold values from 0 to 8191
- field: bfloat16 [8192, 8192], P('row', 'col'), may hold values from -6 to 6
Outputs:
- posterior: bfloat16 [16384, 8192], P('row', 'col')
Inputs may be any that keep to these rules, and one draw needn't show every extreme that they name: `neighbours`: each entry names a row of sim_summaries.
All inputs are finite; a program needn't handle non-finite values.
Results may differ from a plain program's by a relative error of at most 0.005.
Values may be sent and summed in bfloat16 or wider, within the bound.
A program may use at most 128 MiB of HBM per device.

v0:
```python
import jax
import jax.numpy as jnp
from jax import lax
from jax.sharding import PartitionSpec as P

SHARPNESS = 32.0
EPSILON = 1e-06


def neighbour_widths(obs_rows, index_rows, sims_full, sim_square):
    obs_float = obs_rows.astype(jnp.float32)
    near_rows = jnp.take(sims_full, index_rows, axis=0).astype(jnp.float32)
    inner_prod = jnp.einsum("rd,rkd->rk", obs_float, near_rows)
    obs_square = jnp.sum(obs_float * obs_float, axis=1)
    near_square = jnp.take(sim_square, index_rows, axis=0)
    distance = obs_square[:, None] + near_square - 2.0 * inner_prod
    return jnp.mean(distance, axis=1) + EPSILON


def per_device(obs_summaries, sim_summaries, neighbours, field):
    sims_full = lax.all_gather(sim_summaries, "row", axis=0, tiled=True)
    sim_float = sims_full.astype(jnp.float32)
    sim_square = jnp.sum(sim_float * sim_float, axis=1)
    obs_block = lax.all_gather(obs_summaries, "col", axis=0, tiled=True)
    index_block = lax.all_gather(neighbours, "col", axis=0, tiled=True)
    width = neighbour_widths(obs_block, index_block, sims_full, sim_square)
    obs_float = obs_block.astype(jnp.float32)
    obs_square = jnp.sum(obs_float * obs_float, axis=1)
    cross = lax.dot_general(
        obs_block, sims_full, (((1,), (1,)), ((), ())), preferred_element_type=jnp.float32
    )
    distance = obs_square[:, None] + sim_square[None, :] - 2.0 * cross
    weight = jnp.exp(-SHARPNESS * distance / width[:, None])
    numer = jnp.dot(
        weight.astype(jnp.bfloat16),
        lax.all_gather(field, "row", axis=0, tiled=True),
        preferred_element_type=jnp.float32,
    )
    total = jnp.sum(weight, axis=1)
    numer, total = (numer, total)
    return (numer / total[:, None]).astype(jnp.bfloat16)


def solution(mesh):
    return jax.shard_map(
        per_device,
        mesh=mesh,
        in_specs=(
            P(("row", "col"), None),
            P("row", None),
            P(("row", "col"), None),
            P("row", "col"),
        ),
        out_specs=P("row", "col"),
        check_vma=False,
    )
```

profile of v0, /device:TPU:1, one launch (start us, length us, event | category | flops | bytes accessed | tf_op | source)
XLA Modules:
  0.0 260.9 jit_solution(11695345352077202125)
XLA Ops:
  6.5 0.0 all-gather.4.cloned.1.call-start
  6.5 0.7 all-gather.4.cloned.1.call-update
  7.3 0.0 all-gather.6.cloned.1.call-start
  7.3 0.7 all-gather.6.cloned.1.call-update
  8.0 23.7 %all-gather = s32[8,64,16]{1,2,0:T(8,128)S(1)} all-gather(s32[1,64,16]{1,2,0:T(8,128)} %bitcast.17), channel_id=1, replica_groups=mesh['row'=32,'col'=8] {'col'}, dimensions={0}, use_global_device_ids=true | all-gather | bytes 36864 | tf_op jit(solution)/shard_map/all_gather | solution.py:25
  31.7 0.1 reshape.33
  31.8 0.1 copy.10
  31.9 0.1 reshape.14
  32.1 0.2 copy.12
  32.3 22.7 %all_gather.12 = bf16[512,256]{1,0:T(8,128)(2,1)S(1)} all-gather(bf16[64,256]{1,0:T(8,128)(2,1)} %param.4), channel_id=1, replica_groups=mesh['row'=32,'col'=8] {'col'}, dimensions={0}, use_global_device_ids=true | all-gather | bytes 294912 | tf_op jit(solution)/shard_map/all_gather | solution.py:24
  55.0 0.1 multiply_reduce_fusion.1
  55.2 46.5 %all-gather.4.cloned.1.call-done = bf16[8192,256]{1,0:T(8,128)(2,1)} async-done(((bf16[256,256]{1,0:T(8,128)(2,1)}), bf16[8192,256]{1,0:T(8,128)(2,1)}) %all-gather.4.cloned.1.call-update) | async-done | bytes 4194320 | tf_op jit(solution)/shard_map/all_gather | solution.py:21
  101.7 33.6 %gather_fusion.1 = bf16[8192,256]{1,0:T(8,128)(2,1)} fusion(bf16[8192,256]{1,0:T(8,128)(2,1)} %all-gather.4.cloned.1.call-done, s32[8192]{0:T(1024)S(1)} %broadcast_clamp_fusion), kind=kCustom, calls=%fused_computation.1 | custom fusion | bytes 8421376 | tf_op jit(solution)/shard_map/jit(_take)/gather | solution.py:12
  135.3 5.7 %fusion.2 = f32[512,1,16]{2,1,0:T(1,128)S(1)} fusion(bf16[512,16,256]{2,1,0:T(8,128)(2,1)} %bitcast.15, pred[512,16]{1,0:T(8,128)(4,1)S(1)} %copy.12, bf16[512,256,1]{1,0,2:T(8,128)(2,1)S(1)} %bitcast.16), kind=kOutput, calls=%fused_computation.6 | convolution fusion | flops 6291456 | bytes 4497408 | tf_op jit(solution)/shard_map/rd,rkd->rk/dot_general | solution.py:13
  141.0 0.1 copy.14
  141.1 3.4 %multiply_reduce_fusion = f32[8192]{0:T(1024)S(1)} fusion(bf16[8192,256]{1,0:T(8,128)(2,1)} %all-gather.4.cloned.1.call-done), kind=kLoop, calls=%fused_computation.5 | loop fusion | flops 6283264 | bytes 4227072 | tf_op jit(solution)/shard_map/reduce_sum | solution.py:23
  144.4 45.5 %gather_fusion = f32[8192]{0:T(1024)S(1)} fusion(f32[8192]{0:T(1024)S(1)} %multiply_reduce_fusion, s32[8192]{0:T(1024)S(1)} %broadcast_clamp_fusion), kind=kCustom, calls=%fused_computation | custom fusion | bytes 98304 | tf_op jit(solution)/shard_map/jit(_take)/gather | solution.py:15
  190.0 0.1 reshape.13
  190.1 0.1 copy.11
  190.3 10.0 %fusion.12 = (f32[512]{0:T(512)S(1)}, bf16[512,8192]{1,0:T(8,128)(2,1)}) fusion(f32[512]{0:T(512)S(1)} %multiply_add_fusion, bf16[512,256]{1,0:T(8,128)(2,1)S(1)} %all_gather.12, bf16[8192,256]{1,0:T(8,128)(2,1)} %all-gather.4.cloned.1.call-done, f32[8192]{0:T(1024)S(1)} %multiply_reduce_fusion, f32[512]{0:T(512)S(1)} %multiply_reduce_fusion.1), kind=kOutput, calls=%fused_computation.21 | convolution fusion | flops 2176843264 | bytes 12883968 | tf_op jit(solution)/shard_map/dot_general | solution.py:29
  200.2 38.2 %all-gather.6.cloned.1.call-done = bf16[8192,1024]{1,0:T(8,128)(2,1)} async-done(((bf16[256,1024]{1,0:T(8,128)(2,1)}), bf16[8192,1024]{1,0:T(8,128)(2,1)}) %all-gather.6.cloned.1.call-update) | async-done | bytes 16777232 | tf_op jit(solution)/shard_map/all_gather | solution.py:36
  238.5 15.6 %divide_convert_fusion = bf16[512,1024]{1,0:T(8,128)(2,1)} fusion(bf16[8192,1024]{1,0:T(8,128)(2,1)} %all-gather.6.cloned.1.call-done, bf16[512,8192]{1,0:T(8,128)(2,1)} %get-tuple-element.6, f32[512]{0:T(512)S(1)} %get-tuple-element.5), kind=kOutput, calls=%fused_computation.9 | convolution fusion | flops 8590983168 | bytes 26216448 | tf_op jit(solution)/shard_map/dot_general | solution.py:34
  (6 shorter events, 0.1 us)
Async XLA Ops:
  6.5 95.2 %all-gather.4.cloned.1.call-start = ((), (), s32[]{:S(2)}) async-start(), calls=%async_computation | async-start | bytes 4325376 | tf_op jit(solution)/shard_map/all_gather | solution.py:21
  7.3 231.2 %all-gather.6.cloned.1.call-start = ((), (), s32[]{:S(2)}) async-start(), calls=%async_computation.1 | async-start | bytes 17301504 | tf_op jit(solution)/shard_map/all_gather | solution.py:36
Sparse Core Ops, SparseCore 0:
  10.1 91.5 all-gather.3
  104.5 133.9 all-gather.5
where the time goes:
time: 261 us
  waiting for transfers between devices  86.2 us (33%)
  local copies, waits for them, and re-layouts  80 us (31%)
  blocking collectives  46.4 us (18%)
  matrix products  31.2 us (12%)
  between operations  13.5 us (5%)
  other arithmetic  3.58 us (1%)
    all_gather x1, waiting for transfers between devices, per_device(): sims_full = lax.all_gather(sim_summaries, 'row', axis=0, tiled=True)  46.5 us
    gather x3, local copies, waits for them, and re-layouts, neighbour_widths(): near_square = jnp.take(sim_square, index_rows, axis=0)  45.8 us
    all_gather x1, waiting for transfers between devices, per_device(): lax.all_gather(field, 'row', axis=0, tiled=True)  38.2 us
    gather x1, local copies, waits for them, and re-layouts, neighbour_widths(): near_rows = jnp.take(sims_full, index_rows, axis=0).astype(jnp.float32)  33.6 us
    all_gather x1, blocking collectives, per_device(): index_block = lax.all_gather(neighbours, 'col', axis=0, tiled=True)  23.7 us
    all_gather x1, blocking collectives, per_device(): obs_block = lax.all_gather(obs_summaries, 'col', axis=0, tiled=True)  22.7 us
    dot_general x1, matrix products, per_device(): jnp.dot(weight.astype(jnp.bfloat16), lax.all_gather(field, 'row', axis=0,...  15.6 us
    dot_general x1, matrix products, per_device(): lax.dot_general(obs_block, sims_full, (((1,), (1,)), ((), ())), preferred...  9.97 us
  transfers between devices with their start and end apart: 2, of which 2 were waited for; matrix products, arithmetic and copies ran while one was open for 38% of the time, Pallas kernels for 0%

commit v1 on v0

--- a/solution.py
+++ b/solution.py
@@ -5,6 +5,13 @@
 
 SHARPNESS = 32.0
 EPSILON = 1e-06
+
+
+def exchange_gather(x, mesh_axis, along):
+    peers = lax.axis_size(mesh_axis)
+    parts = jnp.stack([x for _ in range(peers)])
+    parts = lax.all_to_all(parts, mesh_axis, split_axis=0, concat_axis=0)
+    return jnp.concatenate(parts, axis=along)
 
 
 def neighbour_widths(obs_rows, index_rows, sims_full, sim_square):
@@ -33,7 +40,7 @@
     weight = jnp.exp(-SHARPNESS * distance / width[:, None])
     numer = jnp.dot(
         weight.astype(jnp.bfloat16),
-        lax.all_gather(field, "row", axis=0, tiled=True),
+        exchange_gather(field, "row", 0),
         preferred_element_type=jnp.float32,
     )
     total = jnp.sum(weight, axis=1)

time: 261 us -> 429 us (1.64); the launches traced: 261 us -> 422 us
  waiting for transfers between devices: 86.2 us -> 226 us
  starting transfers between devices: 0.04 us -> 13 us
  local copies, waits for them, and re-layouts: 80 us -> 86.8 us
    all_to_all x0 -> x1, waiting for transfers between devices: none -> 145 us  [exchange_gather(): parts = lax.all_to_all(parts, mesh_axis, split_axis=0, concat_axis=0)]
    all_gather x1 -> x0, waiting for transfers between devices: 38.2 us -> none  [per_device(): lax.all_gather(field, 'row', axis=0, tiled=True)]
    all_gather x1, waiting for transfers between devices: 46.5 us -> 80 us  [per_device(): sims_full = lax.all_gather(sim_summaries, 'row', axis=0, tiled=True)]
    all_to_all x0 -> x1, starting transfers between devices: none -> 12.9 us  [exchange_gather(): parts = lax.all_to_all(parts, mesh_axis, split_axis=0, concat_axis=0)]
    another operation x0 -> x1, local copies, waits for them, and re-layouts: none -> 6.79 us  [exchange_gather(): parts = jnp.stack([x for _ in range(peers)])]
  transfers between devices with their start and end apart: 2 -> 2, of which waited for: 2 -> 2; matrix products, arithmetic and copies ran while one was open for 38% -> 23% of each run, Pallas kernels for 0% -> 0%
where the time goes in v1:
time: 429 us; the launch traced here: 422 us
  waiting for transfers between devices  226 us (53%)
  local copies, waits for them, and re-layouts  86.8 us (20%)
  blocking collectives  48.5 us (11%)
  matrix products  31.1 us (7%)
  between operations  13.5 us (3%)
  starting transfers between devices  13 us (3%)
    all_to_all x1, waiting for transfers between devices, exchange_gather(): parts = lax.all_to_all(parts, mesh_axis, split_axis=0, concat_axis=0)  145 us
    all_gather x1, waiting for transfers between devices, per_device(): sims_full = lax.all_gather(sim_summaries, 'row', axis=0, tiled=True)  80 us
    gather x3, local copies, waits for them, and re-layouts, neighbour_widths(): near_square = jnp.take(sim_square, index_rows, axis=0)  45.8 us
    gather x1, local copies, waits for them, and re-layouts, neighbour_widths(): near_rows = jnp.take(sims_full, index_rows, axis=0).astype(jnp.float32)  33.6 us
    all_gather x1, blocking collectives, per_device(): index_block = lax.all_gather(neighbours, 'col', axis=0, tiled=True)  24.5 us
    all_gather x1, blocking collectives, per_device(): obs_block = lax.all_gather(obs_summaries, 'col', axis=0, tiled=True)  24.1 us
    dot_general x1, matrix products, per_device(): jnp.dot(weight.astype(jnp.bfloat16), exchange_gather(field, 'row', 0), pr...  15.6 us
    all_to_all x1, starting transfers between devices, exchange_gather(): parts = lax.all_to_all(parts, mesh_axis, split_axis=0, concat_axis=0)  12.9 us
  transfers between devices with their start and end apart: 2, of which 2 were waited for; matrix products, arithmetic and copies ran while one was open for 23% of the time, Pallas kernels for 0%

profile of v1, /device:TPU:1, one launch (start us, length us, event | category | flops | bytes accessed | tf_op | source)
XLA Modules:
  0.0 422.3 jit_solution(12646992926015121760)
XLA Ops:
  6.5 6.8 %stack.2 = bf16[32,256,1024]{2,1,0:T(8,128)(2,1)} broadcast(bf16[256,1024]{1,0:T(8,128)(2,1)} %param.7), dimensions={1,2} | broadcast | bytes 17301504 | tf_op jit(solution)/shard_map/stack | solution.py:12
  13.3 0.0 copy-start.1
  13.3 0.0 copy-start
  13.3 12.9 %all-to-all-start = ((bf16[32,256,1024]{2,1,0:T(8,128)(2,1)}), bf16[32,256,1024]{2,1,0:T(8,128)(2,1)}, u32[]{:S(2)}, u32[]{:S(2)}) async-start(bf16[32,256,1024]{2,1,0:T(8,128)(2,1)} %stack.2), calls=%async_computation | async-start | bytes 33554432 | tf_op jit(solution)/shard_map/all_to_all | solution.py:13
  26.3 0.0 all-gather.3.cloned.1.call-start
  26.3 0.7 all-gather.3.cloned.1.call-update
  27.0 0.0 copy-done.1
  27.0 24.5 %all-gather = s32[8,64,16]{1,2,0:T(8,128)S(1)} all-gather(s32[1,64,16]{1,2,0:T(8,128)S(1)} %bitcast.18), channel_id=1, replica_groups=mesh['row'=32,'col'=8] {'col'}, dimensions={0}, use_global_device_ids=true | all-gather | bytes 36864 | tf_op jit(solution)/shard_map/all_gather | solution.py:32
  51.5 0.1 reshape.39
  51.6 0.1 copy.10
  51.7 0.1 reshape.20
  51.9 0.2 copy.12
  52.1 0.0 copy-done
  52.1 24.1 %all_gather.9 = bf16[512,256]{1,0:T(8,128)(2,1)S(1)} all-gather(bf16[64,256]{1,0:T(8,128)(2,1)S(1)} %copy-done), channel_id=1, replica_groups=mesh['row'=32,'col'=8] {'col'}, dimensions={0}, use_global_device_ids=true | all-gather | bytes 294912 | tf_op jit(solution)/shard_map/all_gather | solution.py:31
  76.2 0.1 multiply_reduce_fusion.1
  76.3 80.0 %all-gather.3.cloned.1.call-done = bf16[8192,256]{1,0:T(8,128)(2,1)} async-done(((bf16[256,256]{1,0:T(8,128)(2,1)}), bf16[8192,256]{1,0:T(8,128)(2,1)}) %all-gather.3.cloned.1.call-update) | async-done | bytes 4194320 | tf_op jit(solution)/shard_map/all_gather | solution.py:28
  156.3 33.6 %gather_fusion.1 = bf16[8192,256]{1,0:T(8,128)(2,1)} fusion(bf16[8192,256]{1,0:T(8,128)(2,1)} %all-gather.3.cloned.1.call-done, s32[8192]{0:T(1024)S(1)} %broadcast_clamp_fusion), kind=kCustom, calls=%fused_computation.1 | custom fusion | bytes 8421376 | tf_op jit(solution)/shard_map/jit(_take)/gather | solution.py:19
  189.9 5.6 %fusion.2 = f32[512,1,16]{2,1,0:T(1,128)S(1)} fusion(bf16[512,16,256]{2,1,0:T(8,128)(2,1)} %bitcast.16, pred[512,16]{1,0:T(8,128)(4,1)S(1)} %copy.12, bf16[512,256,1]{1,0,2:T(8,128)(2,1)S(1)} %bitcast.17), kind=kOutput, calls=%fused_computation.6 | convolution fusion | flops 6291456 | bytes 4497408 | tf_op jit(solution)/shard_map/rd,rkd->rk/dot_general | solution.py:20
  195.6 0.1 copy.14
  195.7 3.4 multiply_reduce_fusion
  199.0 45.5 %gather_fusion = f32[8192]{0:T(1024)S(1)} fusion(f32[8192]{0:T(1024)S(1)} %multiply_reduce_fusion, s32[8192]{0:T(1024)S(1)} %broadcast_clamp_fusion), kind=kCustom, calls=%fused_computation | custom fusion | bytes 98304 | tf_op jit(solution)/shard_map/jit(_take)/gather | solution.py:22
  244.6 0.1 reshape.19
  244.7 0.1 copy.11
  244.8 9.9 %fusion.12 = (f32[512]{0:T(512)S(1)}, bf16[512,8192]{1,0:T(8,128)(2,1)}) fusion(f32[512]{0:T(512)S(1)} %multiply_add_fusion, bf16[512,256]{1,0:T(8,128)(2,1)S(1)} %all_gather.9, bf16[8192,256]{1,0:T(8,128)(2,1)} %all-gather.3.cloned.1.call-done, f32[8192]{0:T(1024)S(1)} %multiply_reduce_fusion, f32[512]{0:T(512)S(1)} %multiply_reduce_fusion.1), kind=kOutput, calls=%fused_computation.21 | convolution fusion | flops 2176843264 | bytes 12883968 | tf_op jit(solution)/shard_map/dot_general | solution.py:36
  254.8 145.1 %all-to-all-done = bf16[32,256,1024]{2,1,0:T(8,128)(2,1)} async-done(((bf16[32,256,1024]{2,1,0:T(8,128)(2,1)}), bf16[32,256,1024]{2,1,0:T(8,128)(2,1)}, u32[]{:S(2)}, u32[]{:S(2)}) %all-to-all-start) | async-done | bytes 16777248 | tf_op jit(solution)/shard_map/all_to_all | solution.py:13
  399.9 15.6 %divide_convert_fusion = bf16[512,1024]{1,0:T(8,128)(2,1)} fusion(bf16[8192,1024]{1,0:T(8,128)(2,1)} %bitcast.4, bf16[512,8192]{1,0:T(8,128)(2,1)} %get-tuple-element.6, f32[512]{0:T(512)S(1)} %get-tuple-element.5), kind=kOutput, calls=%fused_computation.9 | convolution fusion | flops 8590983168 | bytes 26216448 | tf_op jit(solution)/shard_map/dot_general | solution.py:41
  (6 shorter events, 0.1 us)
Async XLA Ops:
  13.3 13.7 %copy-start.1 = (s32[64,16]{0,1:T(8,128)S(1)}, s32[64,16]{0,1:T(8,128)}, u32[]{:S(2)}) copy-start(s32[64,16]{0,1:T(8,128)} %param.6) | copy-start | bytes 12292
  13.3 38.7 %copy-start = (bf16[64,256]{1,0:T(8,128)(2,1)S(1)}, bf16[64,256]{1,0:T(8,128)(2,1)}, u32[]{:S(2)}) copy-start(bf16[64,256]{1,0:T(8,128)(2,1)} %param.4) | copy-start | bytes 98308
  13.3 386.5 %all-to-all-start = ((bf16[32,256,1024]{2,1,0:T(8,128)(2,1)}), bf16[32,256,1024]{2,1,0:T(8,128)(2,1)}, u32[]{:S(2)}, u32[]{:S(2)}) async-start(bf16[32,256,1024]{2,1,0:T(8,128)(2,1)} %stack.2), calls=%async_computation | async-start | bytes 33554432 | tf_op jit(solution)/shard_map/all_to_all | solution.py:13
  26.3 130.0 %all-gather.3.cloned.1.call-start = ((), (), s32[]{:S(2)}) async-start(), calls=%async_computation.1 | async-start | bytes 4325376 | tf_op jit(solution)/shard_map/all_gather | solution.py:28
Sparse Core Ops, SparseCore 0:
  29.9 126.3 all-gather.2
